TPU v7x, 256 devices: a whole 4x4x8 slice. The times are simulated.
256 devices in a mesh: rows: 32 (over y, x, z_lo), tm: 8 (over z_hi, core).
Axes of the slice: x: 4, y: 4, z: 8 (z_hi: 4, z_lo: 2; z = z_hi * 2 + z_lo), core: 2. Of those that a mesh axis runs over, the one named last changes fastest.
Arguments:
- video: bfloat16 [32, 128, 96, 192], P('tm', 'rows'), may hold values from -6 to 6
- gains: float32 [4, 192], replicated, may hold values from 0.1 to 1.9
- kernels: bfloat16 [4, 3, 3, 3, 192, 192], replicated, may hold values from -0.078125 to 0.078125
Outputs:
- encoded: bfloat16 [32, 128, 96, 192], P('tm', 'rows')
All inputs are finite; a program needn't handle non-finite values.
Results may differ from a plain program's by a relative error of at most 0.0065.
Values may be sent and summed in bfloat16 or wider, within the bound.
A program may use at most 128 MiB of HBM per device.

v0:
```python
import jax
import jax.numpy as jnp
from jax import lax
from jax.sharding import PartitionSpec as P


def from_behind(value, axis, steps):
    count = lax.axis_size(axis)
    leading, last = (max(0, -steps), min(count, count - steps))
    return lax.ppermute(value, axis, [(source, source + steps) for source in range(leading, last)])


def extended(block, sides, width):
    for axis, dim in sides:
        count = lax.axis_size(axis)
        forward = [(i, i + 1) for i in range(count - 1)]
        backward = [(target, source) for source, target in forward]
        low = lax.ppermute(
            lax.slice_in_dim(block, block.shape[dim] - width, None, axis=dim), axis, forward
        )
        high = lax.ppermute(lax.slice_in_dim(block, 0, width, axis=dim), axis, backward)
        block = jnp.concatenate([low, block, high], axis=dim)
    return block


def activate(field, gain):
    values = field.astype(jnp.float32)
    scaled = values * lax.rsqrt(jnp.mean(values * values, axis=-1, keepdims=True) + 1e-06) * gain
    return jax.nn.silu(scaled).astype(jnp.bfloat16)


def convolve(field, kernel):
    result = lax.conv_general_dilated(
        field[None],
        kernel,
        (1, 1, 1),
        [(0, 0), (0, 0), (1, 1)],
        dimension_numbers=("NDHWC", "DHWIO", "NDHWC"),
        preferred_element_type=jnp.float32,
    )
    return result[0]


def extend(field):
    before = from_behind(field[-2:], "tm", 1)
    longer = jnp.concatenate([before, field], axis=0)
    return extended(longer, (("rows", 1),), 1)


def body(video, gains, kernels):
    hidden = video
    for block in range(2):
        first = activate(hidden, gains[2 * block])
        second = activate(convolve(extend(first), kernels[2 * block]), gains[2 * block + 1])
        ready = extend(second)
        branch = convolve(ready, kernels[2 * block + 1])
        hidden = (hidden.astype(jnp.float32) + branch).astype(jnp.bfloat16)
    return hidden


def solution(mesh):
    in_specs = (P("tm", "rows", None, None), P(), P())
    out_specs = P("tm", "rows", None, None)
    return jax.shard_map(body, mesh=mesh, in_specs=in_specs, out_specs=out_specs, check_vma=False)
```

profile of v0, /device:TPU:90, one launch (start us, length us, event | category | flops | bytes accessed | tf_op | source)
XLA Modules:
  0.0 181.1 jit_solution(15537369777095429552)
XLA Ops:
  0.0 0.8 fusion.97
  0.8 1.8 %fusion.40 = f32[4,4,96]{1,2,0:T(8,128)S(1)} fusion(bf16[4,4,96,192]{3,2,1,0:T(8,128)(2,1)} %param.3), kind=kLoop, calls=%fused_computation.51 | loop fusion | flops 883200 | bytes 595968 | tf_op jit(solution)/shard_map/reduce_sum | solution.py:28
  2.7 2.4 %fusion.45 = bf16[4,4,96,192]{3,1,2,0:T(4,128)(2,1)S(1)} fusion(f32[192]{0:T(256)S(1)} %bitcast.94, f32[4,4,96]{1,2,0:T(8,128)S(1)} %add_rsqrt_fusion.3, bf16[4,4,96,192]{3,2,1,0:T(8,128)(2,1)} %param.3), kind=kLoop, calls=%fused_computation.56 | loop fusion | flops 2359296 | bytes 1186560 | tf_op jit(solution)/shard_map/convert_element_type | solution.py:29
  5.3 1.9 %collective-permute-start = (bf16[2,4,96,192]{3,1,2,0:T(4,128)(2,1)S(1)}, bf16[2,4,96,192]{3,1,2,0:T(4,128)(2,1)S(1)}, u32[]{:S(2)}, u32[]{:S(2)}) collective-permute-start(bf16[2,4,96,192]{3,1,2,0:T(4,128)(2,1)S(1)} %slice.88), channel_id=1, source_target_pairs={{0,1},{1,2},{2,3},{3,4},{4,5},{5,6},{6,7},{8,9},{9,10},{10,11},{11... | collective-permute-start | bytes 884744 | tf_op jit(solution)/shard_map/ppermute | solution.py:10
  7.2 8.8 %collective-permute-done = bf16[2,4,96,192]{3,1,2,0:T(4,128)(2,1)S(1)} collective-permute-done((bf16[2,4,96,192]{3,1,2,0:T(4,128)(2,1)S(1)}, bf16[2,4,96,192]{3,1,2,0:T(4,128)(2,1)S(1)}, u32[]{:S(2)}, u32[]{:S(2)}) %collective-permute-start) | collective-permute-done | bytes 294944 | tf_op jit(solution)/shard_map/ppermute | solution.py:10
  16.0 1.2 fusion.83
  17.2 7.0 %collective-permute-start.2 = (bf16[6,1,96,192]{3,2,1,0:T(8,128)(2,1)S(1)}, bf16[6,1,96,192]{3,2,1,0:T(8,128)(2,1)S(1)}, u32[]{:S(2)}, u32[]{:S(2)}) collective-permute-start(bf16[6,1,96,192]{3,2,1,0:T(8,128)(2,1)S(1)} %copy.98), channel_id=1, source_target_pairs={{8,0},{16,8},{24,16},{32,24},{40,32},{48,40},{56,48},{64,56},{72,6... | collective-permute-start | bytes 663560 | tf_op jit(solution)/shard_map/ppermute | solution.py:21
  24.2 2.1 %collective-permute-start.1 = (bf16[6,1,96,192]{3,2,1,0:T(8,128)(2,1)S(1)}, bf16[6,1,96,192]{3,2,1,0:T(8,128)(2,1)S(1)}, u32[]{:S(2)}, u32[]{:S(2)}) collective-permute-start(bf16[6,1,96,192]{3,2,1,0:T(8,128)(2,1)S(1)} %copy.97), channel_id=1, source_target_pairs={{0,8},{8,16},{16,24},{24,32},{32,40},{40,48},{48,56},{56,64},{64,7... | collective-permute-start | bytes 663560 | tf_op jit(solution)/shard_map/ppermute | solution.py:18
  26.4 5.2 %collective-permute-done.2 = bf16[6,1,96,192]{3,2,1,0:T(8,128)(2,1)S(1)} collective-permute-done((bf16[6,1,96,192]{3,2,1,0:T(8,128)(2,1)S(1)}, bf16[6,1,96,192]{3,2,1,0:T(8,128)(2,1)S(1)}, u32[]{:S(2)}, u32[]{:S(2)}) %collective-permute-start.2) | collective-permute-done | bytes 221216 | tf_op jit(solution)/shard_map/ppermute | solution.py:21
  32.0 5.7 %collective-permute-done.1 = bf16[6,1,96,192]{3,2,1,0:T(8,128)(2,1)S(1)} collective-permute-done((bf16[6,1,96,192]{3,2,1,0:T(8,128)(2,1)S(1)}, bf16[6,1,96,192]{3,2,1,0:T(8,128)(2,1)S(1)}, u32[]{:S(2)}, u32[]{:S(2)}) %collective-permute-start.1) | collective-permute-done | bytes 221216 | tf_op jit(solution)/shard_map/ppermute | solution.py:18
  38.2 2.3 %maximum_bitcast_fusion = bf16[6,6,1,96,192]{4,1,3,0,2:T(8,128)(2,1)S(1)} fusion(bf16[6,1,96,192]{3,1,2,0:T(2,128)(2,1)S(1)} %copy.100, bf16[4,4,96,192]{3,1,2,0:T(4,128)(2,1)S(1)} %fusion.45, bf16[2,4,96,192]{3,1,2,0:T(4,128)(2,1)S(1)} %collective-permute-done, bf16[6,1,96,192]{3,1,2,0:T(2,128)(2,1)S(1)} %copy.99), kind=kLoop, calls=%fused_computation.23 | loop fusion | flops 5308416 | bytes 2654208 | tf_op jit(solution)/shard_map/broadcast_in_dim | solution.py:34
  42.1 5.4 %fusion.56 = f32[4,4,8,13,192]{4,2,3,1,0:T(8,128)S(1)} fusion(bf16[4,3,3,3,192,192]{5,4,3,2,1,0:T(8,128)(2,1)S(1)} %bitcast.96, bf16[6,6,1,7,2,192]{5,3,4,1,0,2:T(8,128)(2,1)S(1)} %slice.91, bf16[6,6,1,8,13,192]{5,3,4,1,0,2:T(8,128)(2,1)S(1)} %copy.103, pred[8,13]{0,1:T(8,128)(4,1)S(1)} %copy-done.1), kind=kOutput, calls=%fused_computation.73 | convolution fusion | flops 3317747712 | bytes 6146048 | tf_op jit(solution)/shard_map/conv_general_dilated | solution.py:33
  47.6 0.7 copy.104
  48.8 1.1 fusion.54
  50.0 2.3 %collective-permute-start.3 = (bf16[2,4,96,192]{3,1,2,0:T(4,128)(2,1)S(1)}, bf16[2,4,96,192]{3,1,2,0:T(4,128)(2,1)S(1)}, u32[]{:S(2)}, u32[]{:S(2)}) collective-permute-start(bf16[2,4,96,192]{3,1,2,0:T(4,128)(2,1)S(1)} %slice.93), channel_id=1, source_target_pairs={{0,1},{1,2},{2,3},{3,4},{4,5},{5,6},{6,7},{8,9},{9,10},{10,11},{11... | collective-permute-start | bytes 884744 | tf_op jit(solution)/shard_map/ppermute | solution.py:10
  52.3 11.8 %collective-permute-done.3 = bf16[2,4,96,192]{3,1,2,0:T(4,128)(2,1)S(1)} collective-permute-done((bf16[2,4,96,192]{3,1,2,0:T(4,128)(2,1)S(1)}, bf16[2,4,96,192]{3,1,2,0:T(4,128)(2,1)S(1)}, u32[]{:S(2)}, u32[]{:S(2)}) %collective-permute-start.3) | collective-permute-done | bytes 294944 | tf_op jit(solution)/shard_map/ppermute | solution.py:10
  64.2 1.2 fusion.82
  65.4 2.9 %collective-permute-start.5 = (bf16[6,1,96,192]{3,2,1,0:T(8,128)(2,1)S(1)}, bf16[6,1,96,192]{3,2,1,0:T(8,128)(2,1)S(1)}, u32[]{:S(2)}, u32[]{:S(2)}) collective-permute-start(bf16[6,1,96,192]{3,2,1,0:T(8,128)(2,1)S(1)} %copy.108), channel_id=1, source_target_pairs={{8,0},{16,8},{24,16},{32,24},{40,32},{48,40},{56,48},{64,56},{72,6... | collective-permute-start | bytes 663560 | tf_op jit(solution)/shard_map/ppermute | solution.py:21
  68.4 3.2 %collective-permute-start.4 = (bf16[6,1,96,192]{3,2,1,0:T(8,128)(2,1)S(1)}, bf16[6,1,96,192]{3,2,1,0:T(8,128)(2,1)S(1)}, u32[]{:S(2)}, u32[]{:S(2)}) collective-permute-start(bf16[6,1,96,192]{3,2,1,0:T(8,128)(2,1)S(1)} %copy.107), channel_id=1, source_target_pairs={{0,8},{8,16},{16,24},{24,32},{32,40},{40,48},{48,56},{56,64},{64,7... | collective-permute-start | bytes 663560 | tf_op jit(solution)/shard_map/ppermute | solution.py:18
  71.6 5.7 %collective-permute-done.5 = bf16[6,1,96,192]{3,2,1,0:T(8,128)(2,1)S(1)} collective-permute-done((bf16[6,1,96,192]{3,2,1,0:T(8,128)(2,1)S(1)}, bf16[6,1,96,192]{3,2,1,0:T(8,128)(2,1)S(1)}, u32[]{:S(2)}, u32[]{:S(2)}) %collective-permute-start.5) | collective-permute-done | bytes 221216 | tf_op jit(solution)/shard_map/ppermute | solution.py:21
  77.7 5.6 %collective-permute-done.4 = bf16[6,1,96,192]{3,2,1,0:T(8,128)(2,1)S(1)} collective-permute-done((bf16[6,1,96,192]{3,2,1,0:T(8,128)(2,1)S(1)}, bf16[6,1,96,192]{3,2,1,0:T(8,128)(2,1)S(1)}, u32[]{:S(2)}, u32[]{:S(2)}) %collective-permute-start.4) | collective-permute-done | bytes 221216 | tf_op jit(solution)/shard_map/ppermute | solution.py:18
  83.8 2.3 %maximum_bitcast_fusion.1 = bf16[6,6,1,96,192]{4,1,3,0,2:T(8,128)(2,1)S(1)} fusion(bf16[6,1,96,192]{3,1,2,0:T(2,128)(2,1)S(1)} %copy.110, bf16[4,4,96,192]{3,1,2,0:T(4,128)(2,1)S(1)} %fusion.54, bf16[2,4,96,192]{3,1,2,0:T(4,128)(2,1)S(1)} %collective-permute-done.3, bf16[6,1,96,192]{3,1,2,0:T(2,128)(2,1)S(1)} %copy.109), kind=kLoop, calls=%fused_computation.24 | loop fusion | flops 5308416 | bytes 2654208 | tf_op jit(solution)/shard_map/broadcast_in_dim | solution.py:34
  87.1 5.4 %fusion.61 = f32[4,4,8,13,192]{4,2,3,1,0:T(8,128)S(1)} fusion(bf16[4,3,3,3,192,192]{5,4,3,2,1,0:T(8,128)(2,1)S(1)} %bitcast.96, bf16[6,6,1,7,2,192]{5,3,4,1,0,2:T(8,128)(2,1)S(1)} %slice.96, bf16[6,6,1,8,13,192]{5,3,4,1,0,2:T(8,128)(2,1)S(1)} %copy.113, pred[8,13]{0,1:T(8,128)(4,1)S(1)} %copy-done.1), kind=kOutput, calls=%fused_computation.74 | convolution fusion | flops 3317747712 | bytes 6146048 | tf_op jit(solution)/shard_map/conv_general_dilated | solution.py:33
  92.5 0.7 copy.114
  93.7 0.9 fusion.47
  94.6 1.1 fusion.52
  95.9 1.9 %collective-permute-start.6 = (bf16[2,4,96,192]{3,1,2,0:T(4,128)(2,1)S(1)}, bf16[2,4,96,192]{3,1,2,0:T(4,128)(2,1)S(1)}, u32[]{:S(2)}, u32[]{:S(2)}) collective-permute-start(bf16[2,4,96,192]{3,1,2,0:T(4,128)(2,1)S(1)} %slice.98), channel_id=1, source_target_pairs={{0,1},{1,2},{2,3},{3,4},{4,5},{5,6},{6,7},{8,9},{9,10},{10,11},{11... | collective-permute-start | bytes 884744 | tf_op jit(solution)/shard_map/ppermute | solution.py:10
  97.8 12.3 %collective-permute-done.6 = bf16[2,4,96,192]{3,1,2,0:T(4,128)(2,1)S(1)} collective-permute-done((bf16[2,4,96,192]{3,1,2,0:T(4,128)(2,1)S(1)}, bf16[2,4,96,192]{3,1,2,0:T(4,128)(2,1)S(1)}, u32[]{:S(2)}, u32[]{:S(2)}) %collective-permute-start.6) | collective-permute-done | bytes 294944 | tf_op jit(solution)/shard_map/ppermute | solution.py:10
  110.2 1.2 fusion.81
  111.4 2.7 %collective-permute-start.8 = (bf16[6,1,96,192]{3,2,1,0:T(8,128)(2,1)S(1)}, bf16[6,1,96,192]{3,2,1,0:T(8,128)(2,1)S(1)}, u32[]{:S(2)}, u32[]{:S(2)}) collective-permute-start(bf16[6,1,96,192]{3,2,1,0:T(8,128)(2,1)S(1)} %copy.118), channel_id=1, source_target_pairs={{8,0},{16,8},{24,16},{32,24},{40,32},{48,40},{56,48},{64,56},{72,6... | collective-permute-start | bytes 663560 | tf_op jit(solution)/shard_map/ppermute | solution.py:21
  114.2 3.5 %collective-permute-start.7 = (bf16[6,1,96,192]{3,2,1,0:T(8,128)(2,1)S(1)}, bf16[6,1,96,192]{3,2,1,0:T(8,128)(2,1)S(1)}, u32[]{:S(2)}, u32[]{:S(2)}) collective-permute-start(bf16[6,1,96,192]{3,2,1,0:T(8,128)(2,1)S(1)} %copy.117), channel_id=1, source_target_pairs={{0,8},{8,16},{16,24},{24,32},{32,40},{40,48},{48,56},{56,64},{64,7... | collective-permute-start | bytes 663560 | tf_op jit(solution)/shard_map/ppermute | solution.py:18
  117.8 4.9 %collective-permute-done.8 = bf16[6,1,96,192]{3,2,1,0:T(8,128)(2,1)S(1)} collective-permute-done((bf16[6,1,96,192]{3,2,1,0:T(8,128)(2,1)S(1)}, bf16[6,1,96,192]{3,2,1,0:T(8,128)(2,1)S(1)}, u32[]{:S(2)}, u32[]{:S(2)}) %collective-permute-start.8) | collective-permute-done | bytes 221216 | tf_op jit(solution)/shard_map/ppermute | solution.py:21
  123.1 4.8 %collective-permute-done.7 = bf16[6,1,96,192]{3,2,1,0:T(8,128)(2,1)S(1)} collective-permute-done((bf16[6,1,96,192]{3,2,1,0:T(8,128)(2,1)S(1)}, bf16[6,1,96,192]{3,2,1,0:T(8,128)(2,1)S(1)}, u32[]{:S(2)}, u32[]{:S(2)}) %collective-permute-start.7) | collective-permute-done | bytes 221216 | tf_op jit(solution)/shard_map/ppermute | solution.py:18
  128.3 2.3 %maximum_bitcast_fusion.2 = bf16[6,6,1,96,192]{4,1,3,0,2:T(8,128)(2,1)S(1)} fusion(bf16[6,1,96,192]{3,1,2,0:T(2,128)(2,1)S(1)} %copy.120, bf16[4,4,96,192]{3,1,2,0:T(4,128)(2,1)S(1)} %fusion.52, bf16[2,4,96,192]{3,1,2,0:T(4,128)(2,1)S(1)} %collective-permute-done.6, bf16[6,1,96,192]{3,1,2,0:T(2,128)(2,1)S(1)} %copy.119), kind=kLoop, calls=%fused_computation.25 | loop fusion | flops 5308416 | bytes 2654208 | tf_op jit(solution)/shard_map/broadcast_in_dim | solution.py:34
  131.6 5.4 %fusion.66 = f32[4,4,8,13,192]{4,2,3,1,0:T(8,128)S(1)} fusion(bf16[4,3,3,3,192,192]{5,4,3,2,1,0:T(8,128)(2,1)S(1)} %bitcast.96, bf16[6,6,1,7,2,192]{5,3,4,1,0,2:T(8,128)(2,1)S(1)} %slice.101, bf16[6,6,1,8,13,192]{5,3,4,1,0,2:T(8,128)(2,1)S(1)} %copy.123, pred[8,13]{0,1:T(8,128)(4,1)S(1)} %copy-done.1), kind=kOutput, calls=%fused_computation.75 | convolution fusion | flops 3317747712 | bytes 6146048 | tf_op jit(solution)/shard_map/conv_general_dilated | solution.py:33
  137.0 0.7 copy.124
  138.2 1.1 fusion.55
  139.5 1.9 %collective-permute-start.9 = (bf16[2,4,96,192]{3,1,2,0:T(4,128)(2,1)S(1)}, bf16[2,4,96,192]{3,1,2,0:T(4,128)(2,1)S(1)}, u32[]{:S(2)}, u32[]{:S(2)}) collective-permute-start(bf16[2,4,96,192]{3,1,2,0:T(4,128)(2,1)S(1)} %slice.103), channel_id=1, source_target_pairs={{0,1},{1,2},{2,3},{3,4},{4,5},{5,6},{6,7},{8,9},{9,10},{10,11},{11... | collective-permute-start | bytes 884744 | tf_op jit(solution)/shard_map/ppermute | solution.py:10
  141.4 12.0 %collective-permute-done.9 = bf16[2,4,96,192]{3,1,2,0:T(4,128)(2,1)S(1)} collective-permute-done((bf16[2,4,96,192]{3,1,2,0:T(4,128)(2,1)S(1)}, bf16[2,4,96,192]{3,1,2,0:T(4,128)(2,1)S(1)}, u32[]{:S(2)}, u32[]{:S(2)}) %collective-permute-start.9) | collective-permute-done | bytes 294944 | tf_op jit(solution)/shard_map/ppermute | solution.py:10
  153.4 1.2 fusion.80
  154.7 2.2 %collective-permute-start.11 = (bf16[6,1,96,192]{3,2,1,0:T(8,128)(2,1)S(1)}, bf16[6,1,96,192]{3,2,1,0:T(8,128)(2,1)S(1)}, u32[]{:S(2)}, u32[]{:S(2)}) collective-permute-start(bf16[6,1,96,192]{3,2,1,0:T(8,128)(2,1)S(1)} %copy.128), channel_id=1, source_target_pairs={{8,0},{16,8},{24,16},{32,24},{40,32},{48,40},{56,48},{64,56},{72,6... | collective-permute-start | bytes 663560 | tf_op jit(solution)/shard_map/ppermute | solution.py:21
  157.0 3.8 %collective-permute-start.10 = (bf16[6,1,96,192]{3,2,1,0:T(8,128)(2,1)S(1)}, bf16[6,1,96,192]{3,2,1,0:T(8,128)(2,1)S(1)}, u32[]{:S(2)}, u32[]{:S(2)}) collective-permute-start(bf16[6,1,96,192]{3,2,1,0:T(8,128)(2,1)S(1)} %copy.127), channel_id=1, source_target_pairs={{0,8},{8,16},{16,24},{24,32},{32,40},{40,48},{48,56},{56,64},{64,7... | collective-permute-start | bytes 663560 | tf_op jit(solution)/shard_map/ppermute | solution.py:18
  160.8 4.0 %collective-permute-done.11 = bf16[6,1,96,192]{3,2,1,0:T(8,128)(2,1)S(1)} collective-permute-done((bf16[6,1,96,192]{3,2,1,0:T(8,128)(2,1)S(1)}, bf16[6,1,96,192]{3,2,1,0:T(8,128)(2,1)S(1)}, u32[]{:S(2)}, u32[]{:S(2)}) %collective-permute-start.11) | collective-permute-done | bytes 221216 | tf_op jit(solution)/shard_map/ppermute | solution.py:21
  165.2 4.4 %collective-permute-done.10 = bf16[6,1,96,192]{3,2,1,0:T(8,128)(2,1)S(1)} collective-permute-done((bf16[6,1,96,192]{3,2,1,0:T(8,128)(2,1)S(1)}, bf16[6,1,96,192]{3,2,1,0:T(8,128)(2,1)S(1)}, u32[]{:S(2)}, u32[]{:S(2)}) %collective-permute-start.10) | collective-permute-done | bytes 221216 | tf_op jit(solution)/shard_map/ppermute | solution.py:18
  170.1 2.3 %maximum_bitcast_fusion.3 = bf16[6,6,1,96,192]{4,1,3,0,2:T(8,128)(2,1)S(1)} fusion(bf16[6,1,96,192]{3,1,2,0:T(2,128)(2,1)S(1)} %copy.130, bf16[4,4,96,192]{3,1,2,0:T(4,128)(2,1)S(1)} %fusion.55, bf16[2,4,96,192]{3,1,2,0:T(4,128)(2,1)S(1)} %collective-permute-done.9, bf16[6,1,96,192]{3,1,2,0:T(2,128)(2,1)S(1)} %copy.129), kind=kLoop, calls=%fused_computation.26 | loop fusion | flops 5308416 | bytes 2654208 | tf_op jit(solution)/shard_map/broadcast_in_dim | solution.py:34
  173.4 5.4 %fusion.71 = f32[4,4,8,13,192]{4,2,3,1,0:T(8,128)S(1)} fusion(bf16[4,3,3,3,192,192]{5,4,3,2,1,0:T(8,128)(2,1)S(1)} %bitcast.96, bf16[6,6,1,7,2,192]{5,3,4,1,0,2:T(8,128)(2,1)S(1)} %slice.106, bf16[6,6,1,8,13,192]{5,3,4,1,0,2:T(8,128)(2,1)S(1)} %copy.133, pred[8,13]{0,1:T(8,128)(4,1)S(1)} %copy-done.1), kind=kOutput, calls=%fused_computation.76 | convolution fusion | flops 3317747712 | bytes 6146048 | tf_op jit(solution)/shard_map/conv_general_dilated | solution.py:33
  178.8 0.7 copy.134
  179.9 1.0 copy.135
  (50 shorter events, 11.1 us)
Async XLA Ops:
  2.7 38.8 %slice-start = ((s8[10616832]{0:T(1024)(128)(4,1)}), s8[4194304]{0:T(1024)(128)(4,1)S(1)}, s32[]{:S(2)}) async-start(s8[10616832]{0:T(1024)(128)(4,1)} %bitcast.95), calls=%async_computation | async-start | bytes 8388608
  5.3 10.7 %collective-permute-start = (bf16[2,4,96,192]{3,1,2,0:T(4,128)(2,1)S(1)}, bf16[2,4,96,192]{3,1,2,0:T(4,128)(2,1)S(1)}, u32[]{:S(2)}, u32[]{:S(2)}) collective-permute-start(bf16[2,4,96,192]{3,1,2,0:T(4,128)(2,1)S(1)} %slice.88), channel_id=1, source_target_pairs={{0,1},{1,2},{2,3},{3,4},{4,5},{5,6},{6,7},{8,9},{9,10},{10,11},{11... | collective-permute-start | bytes 884744 | tf_op jit(solution)/shard_map/ppermute | solution.py:10
  17.2 14.3 %collective-permute-start.2 = (bf16[6,1,96,192]{3,2,1,0:T(8,128)(2,1)S(1)}, bf16[6,1,96,192]{3,2,1,0:T(8,128)(2,1)S(1)}, u32[]{:S(2)}, u32[]{:S(2)}) collective-permute-start(bf16[6,1,96,192]{3,2,1,0:T(8,128)(2,1)S(1)} %copy.98), channel_id=1, source_target_pairs={{8,0},{16,8},{24,16},{32,24},{40,32},{48,40},{56,48},{64,56},{72,6... | collective-permute-start | bytes 663560 | tf_op jit(solution)/shard_map/ppermute | solution.py:21
  24.2 13.5 %collective-permute-start.1 = (bf16[6,1,96,192]{3,2,1,0:T(8,128)(2,1)S(1)}, bf16[6,1,96,192]{3,2,1,0:T(8,128)(2,1)S(1)}, u32[]{:S(2)}, u32[]{:S(2)}) collective-permute-start(bf16[6,1,96,192]{3,2,1,0:T(8,128)(2,1)S(1)} %copy.97), channel_id=1, source_target_pairs={{0,8},{8,16},{16,24},{24,32},{32,40},{40,48},{48,56},{56,64},{64,7... | collective-permute-start | bytes 663560 | tf_op jit(solution)/shard_map/ppermute | solution.py:18
  32.0 9.5 %slice-start.1 = ((s8[10616832]{0:T(1024)(128)(4,1)}), s8[4194304]{0:T(1024)(128)(4,1)S(1)}, s32[]{:S(2)}) async-start(s8[10616832]{0:T(1024)(128)(4,1)} %bitcast.95), calls=%async_computation.1 | async-start | bytes 8388608
  40.5 1.6 slice-start.2
  41.0 1.1 copy-start.1
  50.0 14.2 %collective-permute-start.3 = (bf16[2,4,96,192]{3,1,2,0:T(4,128)(2,1)S(1)}, bf16[2,4,96,192]{3,1,2,0:T(4,128)(2,1)S(1)}, u32[]{:S(2)}, u32[]{:S(2)}) collective-permute-start(bf16[2,4,96,192]{3,1,2,0:T(4,128)(2,1)S(1)} %slice.93), channel_id=1, source_target_pairs={{0,1},{1,2},{2,3},{3,4},{4,5},{5,6},{6,7},{8,9},{9,10},{10,11},{11... | collective-permute-start | bytes 884744 | tf_op jit(solution)/shard_map/ppermute | solution.py:10
  65.4 11.8 %collective-permute-start.5 = (bf16[6,1,96,192]{3,2,1,0:T(8,128)(2,1)S(1)}, bf16[6,1,96,192]{3,2,1,0:T(8,128)(2,1)S(1)}, u32[]{:S(2)}, u32[]{:S(2)}) collective-permute-start(bf16[6,1,96,192]{3,2,1,0:T(8,128)(2,1)S(1)} %copy.108), channel_id=1, source_target_pairs={{8,0},{16,8},{24,16},{32,24},{40,32},{48,40},{56,48},{64,56},{72,6... | collective-permute-start | bytes 663560 | tf_op jit(solution)/shard_map/ppermute | solution.py:21
  68.4 15.0 %collective-permute-start.4 = (bf16[6,1,96,192]{3,2,1,0:T(8,128)(2,1)S(1)}, bf16[6,1,96,192]{3,2,1,0:T(8,128)(2,1)S(1)}, u32[]{:S(2)}, u32[]{:S(2)}) collective-permute-start(bf16[6,1,96,192]{3,2,1,0:T(8,128)(2,1)S(1)} %copy.107), channel_id=1, source_target_pairs={{0,8},{8,16},{16,24},{24,32},{32,40},{40,48},{48,56},{56,64},{64,7... | collective-permute-start | bytes 663560 | tf_op jit(solution)/shard_map/ppermute | solution.py:18
  92.5 1.1 copy-start
  95.9 14.3 %collective-permute-start.6 = (bf16[2,4,96,192]{3,1,2,0:T(4,128)(2,1)S(1)}, bf16[2,4,96,192]{3,1,2,0:T(4,128)(2,1)S(1)}, u32[]{:S(2)}, u32[]{:S(2)}) collective-permute-start(bf16[2,4,96,192]{3,1,2,0:T(4,128)(2,1)S(1)} %slice.98), channel_id=1, source_target_pairs={{0,1},{1,2},{2,3},{3,4},{4,5},{5,6},{6,7},{8,9},{9,10},{10,11},{11... | collective-permute-start | bytes 884744 | tf_op jit(solution)/shard_map/ppermute | solution.py:10
  111.4 11.2 %collective-permute-start.8 = (bf16[6,1,96,192]{3,2,1,0:T(8,128)(2,1)S(1)}, bf16[6,1,96,192]{3,2,1,0:T(8,128)(2,1)S(1)}, u32[]{:S(2)}, u32[]{:S(2)}) collective-permute-start(bf16[6,1,96,192]{3,2,1,0:T(8,128)(2,1)S(1)} %copy.118), channel_id=1, source_target_pairs={{8,0},{16,8},{24,16},{32,24},{40,32},{48,40},{56,48},{64,56},{72,6... | collective-permute-start | bytes 663560 | tf_op jit(solution)/shard_map/ppermute | solution.py:21
  114.2 13.7 %collective-permute-start.7 = (bf16[6,1,96,192]{3,2,1,0:T(8,128)(2,1)S(1)}, bf16[6,1,96,192]{3,2,1,0:T(8,128)(2,1)S(1)}, u32[]{:S(2)}, u32[]{:S(2)}) collective-permute-start(bf16[6,1,96,192]{3,2,1,0:T(8,128)(2,1)S(1)} %copy.117), channel_id=1, source_target_pairs={{0,8},{8,16},{16,24},{24,32},{32,40},{40,48},{48,56},{56,64},{64,7... | collective-permute-start | bytes 663560 | tf_op jit(solution)/shard_map/ppermute | solution.py:18
  139.5 14.0 %collective-permute-start.9 = (bf16[2,4,96,192]{3,1,2,0:T(4,128)(2,1)S(1)}, bf16[2,4,96,192]{3,1,2,0:T(4,128)(2,1)S(1)}, u32[]{:S(2)}, u32[]{:S(2)}) collective-permute-start(bf16[2,4,96,192]{3,1,2,0:T(4,128)(2,1)S(1)} %slice.103), channel_id=1, source_target_pairs={{0,1},{1,2},{2,3},{3,4},{4,5},{5,6},{6,7},{8,9},{9,10},{10,11},{11... | collective-permute-start | bytes 884744 | tf_op jit(solution)/shard_map/ppermute | solution.py:10
  154.7 10.1 %collective-permute-start.11 = (bf16[6,1,96,192]{3,2,1,0:T(8,128)(2,1)S(1)}, bf16[6,1,96,192]{3,2,1,0:T(8,128)(2,1)S(1)}, u32[]{:S(2)}, u32[]{:S(2)}) collective-permute-start(bf16[6,1,96,192]{3,2,1,0:T(8,128)(2,1)S(1)} %copy.128), channel_id=1, source_target_pairs={{8,0},{16,8},{24,16},{32,24},{40,32},{48,40},{56,48},{64,56},{72,6... | collective-permute-start | bytes 663560 | tf_op jit(solution)/shard_map/ppermute | solution.py:21
  157.0 12.7 %collective-permute-start.10 = (bf16[6,1,96,192]{3,2,1,0:T(8,128)(2,1)S(1)}, bf16[6,1,96,192]{3,2,1,0:T(8,128)(2,1)S(1)}, u32[]{:S(2)}, u32[]{:S(2)}) collective-permute-start(bf16[6,1,96,192]{3,2,1,0:T(8,128)(2,1)S(1)} %copy.127), channel_id=1, source_target_pairs={{0,8},{8,16},{16,24},{24,32},{32,40},{40,48},{48,56},{56,64},{64,7... | collective-permute-start | bytes 663560 | tf_op jit(solution)/shard_map/ppermute | solution.py:18
where the time goes:
time: 184 us; the launch traced here: 181 us
  waiting for transfers between devices  85.3 us (46%)
  starting transfers between devices  35.5 us (19%)
  other arithmetic  23.9 us (13%)
  matrix products  21.7 us (12%)
  local copies, waits for them, and re-layouts  14.1 us (8%)
    ppermute x4, waiting for transfers between devices, from_behind(): lax.ppermute(value, axis, [(source, source + steps) for source in range(l...  45 us
    conv_general_dilated x4, matrix products, convolve(): lax.conv_general_dilated(field[None], kernel, (1, 1, 1), [(0, 0), (0, 0),...  21.7 us
    ppermute x4, waiting for transfers between devices, extended(): lax.ppermute(lax.slice_in_dim(block, block.shape[dim] - width, None, axis...  20.5 us
    ppermute x4, waiting for transfers between devices, extended(): lax.ppermute(lax.slice_in_dim(block, 0, width, axis=dim), axis, backward)  19.8 us
    ppermute x4, starting transfers between devices, extended(): lax.ppermute(lax.slice_in_dim(block, 0, width, axis=dim), axis, backward)  14.7 us
    ppermute x4, starting transfers between devices, extended(): lax.ppermute(lax.slice_in_dim(block, block.shape[dim] - width, None, axis...  12.7 us
    broadcast_in_dim x4, other arithmetic, convolve(): field[None]  9.06 us
    ppermute x4, starting transfers between devices, from_behind(): lax.ppermute(value, axis, [(source, source + steps) for source in range(l...  8.08 us
  transfers between devices with their start and end apart: 12, of which 12 were waited for; matrix products, arithmetic and copies ran while one was open for 1% of the time, Pallas kernels for 0%

commit v1 on v0

v1 whole, which is shorter than its diff:
```python
import jax
import jax.numpy as jnp
from jax import lax
from jax.experimental import pallas as pl
from jax.experimental.pallas import tpu as pltpu
from jax.sharding import PartitionSpec as P

MESH = pl.DeviceIdType.MESH
BF = jnp.bfloat16
F32 = jnp.float32
F, R, W, C = 4, 4, 96, 192
LO, HI = 128, 64
K1 = 640


def norm_act(value, gain):
    lo, hi = value
    mean = jnp.sum(lo * lo + hi * hi, axis=-1, keepdims=True) * (1.0 / C)
    scale = lax.rsqrt(mean + 1e-06)
    return tuple(s / (1.0 + jnp.exp(-s)) for s in (lo * scale * gain[0], hi * scale * gain[1]))


def lane_id():
    return lax.broadcasted_iota(jnp.int32, (W, LO), 1)


def join(first, second):
    both = first[1] + pltpu.roll(second[1], HI, 1)
    return jnp.concatenate([first[0].astype(BF), second[0].astype(BF), both.astype(BF)], axis=1)


def split(packet):
    values = packet.astype(F32)
    tail = values[:, 2 * LO :]
    low = lane_id() < HI
    first = jnp.where(low, tail, 0.0)
    second = jnp.where(low, pltpu.roll(tail, HI, 1), 0.0)
    return (values[:, :LO], first), (values[:, LO : 2 * LO], second)


def widen(ref, value):
    column = lax.broadcasted_iota(jnp.int32, (W, LO), 0)
    lo, hi = value

    def left(v):
        return jnp.where(column == 0, 0.0, pltpu.roll(v, 1, 0))

    def right(v):
        return jnp.where(column == W - 1, 0.0, pltpu.roll(v, W - 1, 0))

    ref[:, 0:128] = left(lo).astype(BF)
    ref[:, 128:256] = lo.astype(BF)
    ref[:, 256:384] = right(lo).astype(BF)
    ref[:, 384:512] = (left(hi) + pltpu.roll(hi, HI, 1)).astype(BF)
    ref[:, 512:640] = right(hi).astype(BF)


def place():
    r, t = lax.axis_index("rows"), lax.axis_index("tm")
    r2, t2 = lax.div(r, 2), lax.div(t, 2)
    r1, t1 = lax.rem(r, 2), lax.rem(t, 2)
    return 2 * t2 + r1, 2 * r2 + t1, (2 * r2 + t1, 2 * t2 + r1), r1 != t1


def device(slab, strip):
    s2, q2 = lax.div(slab, 2), lax.div(strip, 2)
    return 2 * q2 + lax.rem(slab, 2), 2 * s2 + lax.rem(strip, 2)


def kernel(
    video, gains, kernels, out,
    vid, res, X, Wt, acc, own, swap_out, swap_in, A, T, N, Q,
    w_sem, v_sem, l_sem, o_sem, sw_send, sw_recv, t_send, t_recv, n_send, n_recv, q_send, q_recv,
):
    slab, strip, partner, swaps = place()
    has_prev, has_next = slab > 0, slab < 7
    has_up, has_down = strip > 0, strip < 31
    prev, follow = device(slab - 1, strip), device(slab + 1, strip)
    up, down = device(slab, strip - 1), device(slab, strip + 1)

    loads = [pltpu.make_async_copy(video.at[pl.ds(2, 2)], vid.at[pl.ds(2, 2)], v_sem.at[1]),
             pltpu.make_async_copy(video.at[pl.ds(0, 2)], vid.at[pl.ds(0, 2)], v_sem.at[0])]
    for copy in loads:
        copy.start()
    weights = []
    for k in range(4):
        group = [pltpu.make_async_copy(
            kernels.at[k, :, :, :, pl.ds(0, LO), :], Wt.at[k, :, :, pl.ds(0, 3), :, :], w_sem.at[k, 0])]
        for q in range(3):
            group.append(pltpu.make_async_copy(
                kernels.at[k, :, :, q, pl.ds(LO, HI), :],
                Wt.at[k, :, :, 3 + q // 2, pl.ds(HI * (q % 2), HI), :],
                w_sem.at[k, 1 + q]))
        weights.append(group)
    for copy in weights[0]:
        copy.start()

    barrier = pltpu.get_barrier_semaphore()
    count = jnp.int32(0)
    for there, target in ((has_prev, prev), (has_next, follow), (has_up, up), (has_down, down), (swaps, partner)):
        count = count + there.astype(jnp.int32)

        @pl.when(there)
        def _(target=target):
            pl.semaphore_signal(barrier, inc=1, device_id=target, device_id_type=MESH)

    pl.semaphore_wait(barrier, count)

    def remote(src, dst, send, recv, target):
        return pltpu.make_async_remote_copy(
            src_ref=src, dst_ref=dst, send_sem=send, recv_sem=recv, device_id=target, device_id_type=MESH)

    def exchange(source, sink, n, p):
        copy = remote(source.at[p], sink.at[p], sw_send.at[n, p], sw_recv.at[n, p], partner)
        local = pltpu.make_async_copy(source.at[p], sink.at[p], l_sem.at[n, p])
        return copy, local

    def begin(pair):
        copy, local = pair

        @pl.when(swaps)
        def _():
            copy.start()

        @pl.when(jnp.logical_not(swaps))
        def _():
            local.start()

    def finish(pair):
        copy, local = pair

        @pl.when(swaps)
        def _():
            copy.wait_recv()

        @pl.when(jnp.logical_not(swaps))
        def _():
            local.wait()

    inward = {}
    for p, load in ((1, loads[0]), (0, loads[1])):
        load.wait()

        @pl.loop(0, R)
        def _(r, p=p):
            pair = []
            for f in range(2):
                whole = vid[2 * p + f, r].astype(F32)
                whole = jnp.concatenate([whole, jnp.zeros((W, HI), F32)], axis=1)
                pair.append((whole[:, :LO], whole[:, LO:]))
            own[p, r] = join(*pair)

        inward[p] = exchange(own, swap_in, 0, p)
        begin(inward[p])

    for k in range(1, 4):
        for copy in weights[k]:
            copy.start()
    for s in range(2):
        X[s, 0:2] = jnp.zeros((2, R + 2, W, K1), BF)

        @pl.loop(2, F + 2)
        def _(f, s=s):
            X[s, f, 0] = jnp.zeros((W, K1), BF)
            X[s, f, R + 1] = jnp.zeros((W, K1), BF)

    Wt[:, :, :, 4, HI:, :] = jnp.zeros((4, 3, 3, LO - HI, C), BF)

    def gain(k):
        row = jnp.concatenate([gains[k : k + 1, :], jnp.zeros((1, HI), F32)], axis=1)
        return row[:, :LO], row[:, LO:]

    def frames_copy(j, r):
        return remote(A.at[j, 1, r], T.at[j, r], t_send.at[j, r], t_recv.at[j, r], follow)

    def row_copy(j, p, side):
        return remote(A.at[j, p, 3 * side], N.at[j, p, 1 - side], n_send.at[j, p, side], n_recv.at[j, p, 1 - side],
                      (up, down)[side])

    def corner_copy(j, side):
        return remote(T.at[j, 3 * side], Q.at[j, 1 - side], q_send.at[j, side], q_recv.at[j, 1 - side],
                      (up, down)[side])

    def send(j, p):
        for side, there in ((0, has_up), (1, has_down)):
            @pl.when(there)
            def _(side=side):
                row_copy(j, p, side).start()
        if p == 1:
            @pl.when(has_next)
            def _():
                for r in (0, 3, 1, 2):
                    frames_copy(j, r).start()

    def emit(j, p, r, pair):
        for f in range(2):
            widen(X.at[j % 2, 2 + 2 * p + f, r + 1], pair[f])
        A[j, p, r] = join(*pair)

    def widen_packet(ref, j, f, r):
        pair = split(ref[...])
        for i in range(2):
            widen(X.at[j % 2, f + i, r], pair[i])

    def take_rows(j):
        for side, there in ((0, has_up), (1, has_down)):
            @pl.when(there)
            def _(side=side):
                for p in (1, 0):
                    row_copy(j, p, 1 - side).wait_recv()
                    widen_packet(N.at[j, p, side], j, 2 + 2 * p, 5 * side)

    def take_frames(j):
        @pl.when(has_prev)
        def _():
            for side, there in ((0, has_up), (1, has_down)):
                frames_copy(j, 3 * side).wait_recv()

                @pl.when(there)
                def _(side=side):
                    corner_copy(j, side).start()
            for r in (1, 2):
                frames_copy(j, r).wait_recv()

            @pl.loop(0, R)
            def _(r):
                widen_packet(T.at[j, r], j, 0, r + 1)

            for side, there in ((0, has_up), (1, has_down)):
                @pl.when(there)
                def _(side=side):
                    corner_copy(j, 1 - side).wait_recv()
                    widen_packet(Q.at[j, side], j, 0, 5 * side)

    def convolve(j, p):
        s = j % 2
        parts = [X[s, 2 * p + dt : 2 * p + dt + 2, dr : dr + R].reshape(2 * R * W, K1)
                 for dt in range(3) for dr in range(3)]
        acc[...] = jnp.dot(
            jnp.concatenate(parts, axis=1), Wt[j].reshape(9 * K1, C), preferred_element_type=F32
        ).reshape(2, R, W, C)

    def sums(f, r):
        return acc[f, r, :, 0:LO], jnp.concatenate([acc[f, r, :, LO:C], jnp.zeros((W, HI), F32)], axis=1)

    def after(j, p):
        g = gain(j + 1) if j < 3 else None

        @pl.loop(0, R)
        def _(r):
            pair = [sums(f, r) for f in range(2)]
            if j % 2 == 1:
                old = split(swap_in[p, r])
                pair = [tuple((a + b).astype(BF).astype(F32) for a, b in zip(*both)) for both in zip(old, pair)]
                swap_in[p, r] = join(*pair)
            if j < 3:
                emit(j + 1, p, r, [norm_act(v, g) for v in pair])

    g0 = gain(0)
    for p in (1, 0):
        finish(inward[p])

        @pl.loop(0, R)
        def _(r, p=p):
            emit(0, p, r, [norm_act(v, g0) for v in split(swap_in[p, r])])

        send(0, p)

    outward = {}
    for j in range(4):
        take_rows(j)
        for copy in weights[j]:
            copy.wait()
        for p in (1, 0):
            if p == 0:
                take_frames(j)
            convolve(j, p)
            after(j, p)
            if j < 3:
                send(j + 1, p)
            else:
                outward[p] = exchange(swap_in, swap_out, 1, p)
                begin(outward[p])

    stores = []
    for p in (1, 0):
        finish(outward[p])

        @pl.loop(0, R)
        def _(r, p=p):
            pair = split(swap_out[p, r])
            for f in range(2):
                res[2 * p + f, r, :, 0:LO] = pair[f][0].astype(BF)
                res[2 * p + f, r, :, LO:C] = pair[f][1][:, :HI].astype(BF)

        store = pltpu.make_async_copy(res.at[pl.ds(2 * p, 2)], out.at[pl.ds(2 * p, 2)], o_sem.at[p])
        store.start()
        stores.append(store)

    @pl.when(swaps)
    def _():
        for p in (1, 0):
            inward[p][0].wait_send()
            outward[p][0].wait_send()

    for j in range(4):
        for side, there in ((0, has_up), (1, has_down)):
            @pl.when(there)
            def _(j=j, side=side):
                for p in (1, 0):
                    row_copy(j, p, side).wait_send()

                @pl.when(has_prev)
                def _():
                    corner_copy(j, side).wait_send()

        @pl.when(has_next)
        def _(j=j):
            for r in range(R):
                frames_copy(j, r).wait_send()

    for store in stores:
        store.wait()


def body(video, gains, kernels):
    packet = (W, 2 * C)
    dma = pltpu.SemaphoreType.DMA
    return pl.pallas_call(
        kernel,
        out_shape=jax.ShapeDtypeStruct(video.shape, video.dtype),
        in_specs=[
            pl.BlockSpec(memory_space=pl.ANY),
            pl.BlockSpec(memory_space=pltpu.VMEM),
            pl.BlockSpec(memory_space=pl.ANY),
        ],
        out_specs=pl.BlockSpec(memory_space=pl.ANY),
        scratch_shapes=[
            pltpu.VMEM((F, R, W, C), BF),
            pltpu.VMEM((F, R, W, C), BF),
            pltpu.VMEM((2, F + 2, R + 2, W, K1), BF),
            pltpu.VMEM((4, 3, 3, 5, LO, C), BF),
            pltpu.VMEM((2, R, W, C), F32),
            pltpu.VMEM((2, R) + packet, BF),
            pltpu.VMEM((2, R) + packet, BF),
            pltpu.VMEM((2, R) + packet, BF),
            pltpu.VMEM((4, 2, R) + packet, BF),
            pltpu.VMEM((4, R) + packet, BF),
            pltpu.VMEM((4, 2, 2) + packet, BF),
            pltpu.VMEM((4, 2) + packet, BF),
            dma((4, 4)), dma((2,)), dma((2, 2)), dma((2,)),
            dma((2, 2)), dma((2, 2)),
            dma((4, R)), dma((4, R)),
            dma((4, 2, 2)), dma((4, 2, 2)),
            dma((4, 2)), dma((4, 2)),
        ],
        compiler_params=pltpu.CompilerParams(
            collective_id=0, has_side_effects=True, vmem_limit_bytes=56 << 20),
        name="blocks",
    )(video, gains, kernels)


def solution(mesh):
    in_specs = (P("tm", "rows", None, None), P(), P())
    out_specs = P("tm", "rows", None, None)
    return jax.shard_map(body, mesh=mesh, in_specs=in_specs, out_specs=out_specs, check_vma=False)
```

time: 184 us -> 108 us (0.59)
  the two profiles are of different devices: /device:TPU:90 before, /device:TPU:9 now
where the time goes in v1:
time: 108 us
  Pallas kernels  106 us (98%)
  local copies, waits for them, and re-layouts  2.06 us (2%)
    pallas_call x1, Pallas kernels, body(): pl.pallas_call(kernel, out_shape=jax.ShapeDtypeStruct(video.shape, video....  106 us

profile of v1, /device:TPU:9, one launch (start us, length us, event | category | flops | bytes accessed | tf_op | source)
XLA Modules:
  0.0 108.0 jit_solution(4553973098024141549)
XLA Ops:
  0.0 105.9 %blocks.1 = bf16[4,4,96,192]{3,2,1,0:T(8,128)(2,1)} custom-call(bf16[4,4,96,192]{3,2,1,0:T(8,128)(2,1)} %video.1, f32[4,192]{1,0:T(4,128)} %gains.1, bf16[4,3,3,3,192,192]{5,4,3,2,1,0:T(8,128)(2,1)} %kernels.1), custom_call_target="tpu_custom_call" | custom-call | tf_op jit(solution)/shard_map/blocks/pallas_call | solution.py:329
  105.9 2.1 %copy.5 = bf16[4,4,96,192]{3,2,1,0:T(8,128)(2,1)} copy(bf16[4,4,96,192]{3,2,1,0:T(8,128)(2,1)} %blocks.1) | data formatting | bytes 1179648

commit v2 on v1

v2 whole, which is shorter than its diff:
```python
import jax
import jax.numpy as jnp
from jax import lax
from jax.experimental import pallas as pl
from jax.experimental.pallas import tpu as pltpu
from jax.sharding import PartitionSpec as P

MESH = pl.DeviceIdType.MESH
BF = jnp.bfloat16
F32 = jnp.float32
F, R, W, C = 4, 4, 96, 192
LO, HI = 128, 64
K1 = 640


def norm_act(value, gain):
    lo, hi = value
    mean = jnp.sum(lo * lo + hi * hi, axis=-1, keepdims=True) * (1.0 / C)
    scale = lax.rsqrt(mean + 1e-06)
    return tuple(s / (1.0 + jnp.exp(-s)) for s in (lo * scale * gain[0], hi * scale * gain[1]))


def lane_id():
    return lax.broadcasted_iota(jnp.int32, (W, LO), 1)


def join(first, second):
    both = first[1] + pltpu.roll(second[1], HI, 1)
    return jnp.concatenate([first[0].astype(BF), second[0].astype(BF), both.astype(BF)], axis=1)


def split(packet):
    values = packet.astype(F32)
    tail = values[:, 2 * LO :]
    low = lane_id() < HI
    first = jnp.where(low, tail, 0.0)
    second = jnp.where(low, pltpu.roll(tail, HI, 1), 0.0)
    return (values[:, :LO], first), (values[:, LO : 2 * LO], second)


def widen(ref, value):
    column = lax.broadcasted_iota(jnp.int32, (W, LO), 0)
    lo, hi = value

    def left(v):
        return jnp.where(column == 0, 0.0, pltpu.roll(v, 1, 0))

    def right(v):
        return jnp.where(column == W - 1, 0.0, pltpu.roll(v, W - 1, 0))

    ref[:, 0:128] = left(lo).astype(BF)
    ref[:, 128:256] = lo.astype(BF)
    ref[:, 256:384] = right(lo).astype(BF)
    ref[:, 384:512] = (left(hi) + pltpu.roll(hi, HI, 1)).astype(BF)
    ref[:, 512:640] = right(hi).astype(BF)


def place():
    r, t = lax.axis_index("rows"), lax.axis_index("tm")
    r2, t2 = lax.div(r, 2), lax.div(t, 2)
    r1, t1 = lax.rem(r, 2), lax.rem(t, 2)
    return 2 * t2 + r1, 2 * r2 + t1, (2 * r2 + t1, 2 * t2 + r1), r1 != t1


def device(slab, strip):
    s2, q2 = lax.div(slab, 2), lax.div(strip, 2)
    return 2 * q2 + lax.rem(slab, 2), 2 * s2 + lax.rem(strip, 2)


def kernel(
    video, gains, kernels, out,
    vid, res, X, Wt, acc, own, swap_out, swap_in, A, T, N, Q,
    w_sem, v_sem, l_sem, o_sem, sw_send, sw_recv, t_send, t_recv, n_send, n_recv, q_send, q_recv,
):
    slab, strip, partner, swaps = place()
    has_prev, has_next = slab > 0, slab < 7
    has_up, has_down = strip > 0, strip < 31
    prev, follow = device(slab - 1, strip), device(slab + 1, strip)
    up, down = device(slab, strip - 1), device(slab, strip + 1)

    loads = [pltpu.make_async_copy(video.at[pl.ds(2, 2)], vid.at[pl.ds(2, 2)], v_sem.at[1]),
             pltpu.make_async_copy(video.at[pl.ds(0, 2)], vid.at[pl.ds(0, 2)], v_sem.at[0])]
    for copy in loads:
        copy.start()

    def weights(k):
        copies = [pltpu.make_async_copy(
            kernels.at[k, :, :, :, pl.ds(0, LO), :], Wt.at[k, :, :, pl.ds(0, 3), :, :], w_sem.at[k, 0])]
        for q in range(3):
            copies.append(pltpu.make_async_copy(
                kernels.at[k, :, :, q, pl.ds(LO, HI), :],
                Wt.at[k, :, :, 3 + q // 2, pl.ds(HI * (q % 2), HI), :],
                w_sem.at[k, 1 + q]))
        return copies

    zero = jnp.zeros((W, 2 * C), BF)
    for side, there in ((0, has_up), (1, has_down)):
        @pl.when(jnp.logical_not(there))
        def _(side=side):
            @pl.loop(0, 4)
            def _(j):
                N[j, 0, side] = zero
                N[j, 1, side] = zero
                Q[j, side] = zero

    @pl.when(jnp.logical_not(has_prev))
    def _():
        @pl.loop(0, 4)
        def _(j):
            for r in range(R):
                T[j, r] = zero
            for side in range(2):
                Q[j, side] = zero

    barrier = pltpu.get_barrier_semaphore()
    count = jnp.int32(0)
    for there, target in ((has_prev, prev), (has_next, follow), (has_up, up), (has_down, down), (swaps, partner)):
        count = count + there.astype(jnp.int32)

        @pl.when(there)
        def _(target=target):
            pl.semaphore_signal(barrier, inc=1, device_id=target, device_id_type=MESH)

    pl.semaphore_wait(barrier, count)

    def remote(src, dst, send, recv, target):
        return pltpu.make_async_remote_copy(
            src_ref=src, dst_ref=dst, send_sem=send, recv_sem=recv, device_id=target, device_id_type=MESH)

    def exchange(source, sink, n, p, r=None):
        at = (p,) if r is None else (p, r)
        sem = (n, p, 0) if r is None else (n, p, r)
        copy = remote(source.at[at], sink.at[at], sw_send.at[sem], sw_recv.at[sem], partner)
        local = pltpu.make_async_copy(source.at[at], sink.at[at], l_sem.at[sem])
        return copy, local

    def begin(pair):
        copy, local = pair

        @pl.when(swaps)
        def _():
            copy.start()

        @pl.when(jnp.logical_not(swaps))
        def _():
            local.start()

    def finish(pair):
        copy, local = pair

        @pl.when(swaps)
        def _():
            copy.wait_recv()

        @pl.when(jnp.logical_not(swaps))
        def _():
            local.wait()

    def packed(r, p):
        pair = []
        for f in range(2):
            whole = vid[2 * p + f, r].astype(F32)
            whole = jnp.concatenate([whole, jnp.zeros((W, HI), F32)], axis=1)
            pair.append((whole[:, :LO], whole[:, LO:]))
        own[p, r] = join(*pair)

    for q, load in enumerate(loads):
        p = 1 - q
        load.wait()

        @pl.loop(0, R)
        def _(r, p=p):
            packed(r, p)

        begin(exchange(own, swap_in, 0, p))

    for copy in weights(0):
        copy.start()

    @pl.loop(1, 4)
    def _(k):
        for copy in weights(k):
            copy.start()

    @pl.loop(0, 36)
    def _(i):
        Wt[lax.div(i, 9), lax.div(lax.rem(i, 9), 3), lax.rem(i, 3), 4, HI:, :] = jnp.zeros((LO - HI, C), BF)

    def gain(k):
        row = jnp.concatenate([gains[pl.ds(k, 1), :], jnp.zeros((1, HI), F32)], axis=1)
        return row[:, :LO], row[:, LO:]

    def frames_copy(j, r):
        return remote(A.at[j, 1, r], T.at[j, r], t_send.at[j, r], t_recv.at[j, r], follow)

    def row_copy(j, p, side):
        return remote(A.at[j, p, 3 * side], N.at[j, p, 1 - side], n_send.at[j, p, side], n_recv.at[j, p, 1 - side],
                      (up, down)[side])

    def corner_copy(j, side):
        return remote(T.at[j, 3 * side], Q.at[j, 1 - side], q_send.at[j, side], q_recv.at[j, 1 - side],
                      (up, down)[side])

    sides = ((0, has_up), (1, has_down))

    def send_rows(j, p):
        for side, there in sides:
            @pl.when(there)
            def _(side=side):
                row_copy(j, p, side).start()

    def send_frames(j):
        @pl.when(has_next)
        def _():
            for r in (0, 3, 1, 2):
                frames_copy(j, r).start()

    def emit(j, p, r, pair):
        for f in range(2):
            widen(X.at[lax.rem(j, 2), 2 + 2 * p + f, r + 1], pair[f])
        A[j, p, r] = join(*pair)

    def widen_packet(ref, j, f, r):
        pair = split(ref[...])
        for i in range(2):
            widen(X.at[lax.rem(j, 2), f + i, r], pair[i])

    def take_rows(j):
        for side, there in sides:
            @pl.when(there)
            def _(side=side):
                for p in (1, 0):
                    row_copy(j, p, 1 - side).wait_recv()

        @pl.loop(0, 4)
        def _(i):
            p, side = lax.div(i, 2), lax.rem(i, 2)
            widen_packet(N.at[j, p, side], j, 2 + 2 * p, 5 * side)

    def forward_corners(j):
        @pl.when(has_prev)
        def _():
            for side, there in sides:
                frames_copy(j, 3 * side).wait_recv()

                @pl.when(there)
                def _(side=side):
                    corner_copy(j, side).start()

    def take_frames(j):
        @pl.when(has_prev)
        def _():
            for r in (1, 2):
                frames_copy(j, r).wait_recv()

        @pl.loop(0, R)
        def _(r):
            widen_packet(T.at[j, r], j, 0, r + 1)

        for side, there in sides:
            @pl.when(jnp.logical_and(there, has_prev))
            def _(side=side):
                corner_copy(j, 1 - side).wait_recv()

        @pl.loop(0, 2)
        def _(side):
            widen_packet(Q.at[j, side], j, 0, 5 * side)

    def convolve(j, p, rows):
        s = lax.rem(j, 2)
        parts = []
        for dt in range(3):
            for dr in range(3):
                parts.append(jnp.concatenate(
                    [X[s, 2 * p + dt + f, r + dr] for f in range(2) for r in rows], axis=0))
        acc[...] = jnp.dot(
            jnp.concatenate(parts, axis=1), Wt[j].reshape(9 * K1, C), preferred_element_type=F32
        ).reshape(2, 2, W, C)

    def sums(f, i):
        return acc[f, i, :, 0:LO], jnp.concatenate([acc[f, i, :, LO:C], jnp.zeros((W, HI), F32)], axis=1)

    def after(j, p, rows):
        @pl.when(lax.rem(j, 2) == 1)
        def _():
            @pl.loop(0, 2)
            def _(i):
                r = rows[0] + i * (rows[1] - rows[0])
                old = split(swap_in[p, r])
                pair = [tuple((a + b).astype(BF).astype(F32) for a, b in zip(old[f], sums(f, i))) for f in range(2)]
                swap_in[p, r] = join(*pair)
                for f in range(2):
                    acc[f, i, :, 0:LO] = pair[f][0]
                    acc[f, i, :, LO:C] = pair[f][1][:, :HI]

        @pl.when(j < 3)
        def _():
            g = gain(j + 1)

            @pl.loop(0, 2)
            def _(i):
                r = rows[0] + i * (rows[1] - rows[0])
                emit(j + 1, p, r, [norm_act(sums(f, i), g) for f in range(2)])

    def outward(p, r):
        return exchange(swap_in, swap_out, 1, p, r)

    g0 = gain(0)

    @pl.loop(0, 2)
    def _(q):
        p = 1 - q
        finish(exchange(own, swap_in, 0, p))

        @pl.loop(0, R)
        def _(r):
            emit(0, p, r, [norm_act(v, g0) for v in split(swap_in[p, r])])

        send_rows(0, p)

        @pl.when(p == 1)
        def _():
            send_frames(0)

    def unit(u):
        first = jnp.where(jnp.logical_or(u == 1, u == 2), 0, 1)
        return 1 - lax.div(u, 2), (first, 3 - first)

    @pl.loop(0, 4)
    def _(j):
        for copy in weights(j):
            copy.wait()

        @pl.loop(0, 4)
        def _(u):
            p, rows = unit(u)

            @pl.when(u == 1)
            def _():
                take_rows(j)
                forward_corners(j)

            @pl.when(u == 2)
            def _():
                take_frames(j)

            convolve(j, p, rows)
            after(j, p, rows)

            @pl.when(jnp.logical_and(j < 3, jnp.logical_or(u == 1, u == 2)))
            def _():
                send_rows(j + 1, p)

            @pl.when(jnp.logical_and(j < 3, u == 1))
            def _():
                send_frames(j + 1)

            @pl.when(j == 3)
            def _():
                for r in rows:
                    begin(outward(p, r))

    def stored(p, r):
        return pltpu.make_async_copy(res.at[pl.ds(2 * p, 2), r], out.at[pl.ds(2 * p, 2), r], o_sem.at[p, r])

    @pl.loop(0, 8)
    def _(i):
        p, rows = unit(lax.div(i, 2))
        r = rows[0] + lax.rem(i, 2) * (rows[1] - rows[0])
        finish(outward(p, r))
        pair = split(swap_out[p, r])
        for f in range(2):
            res[2 * p + f, r, :, 0:LO] = pair[f][0].astype(BF)
            res[2 * p + f, r, :, LO:C] = pair[f][1][:, :HI].astype(BF)
        stored(p, r).start()

    @pl.when(swaps)
    def _():
        @pl.loop(0, 2)
        def _(p):
            exchange(own, swap_in, 0, p)[0].wait_send()

            @pl.loop(0, R)
            def _(r):
                outward(p, r)[0].wait_send()

    @pl.loop(0, 4)
    def _(j):
        for side, there in sides:
            @pl.when(there)
            def _(side=side):
                for p in (1, 0):
                    row_copy(j, p, side).wait_send()

            @pl.when(jnp.logical_and(there, has_prev))
            def _(side=side):
                corner_copy(j, side).wait_send()

        @pl.when(has_next)
        def _():
            for r in range(R):
                frames_copy(j, r).wait_send()

    @pl.loop(0, 2)
    def _(p):
        @pl.loop(0, R)
        def _(r):
            stored(p, r).wait()


def body(video, gains, kernels):
    packet = (W, 2 * C)
    dma = pltpu.SemaphoreType.DMA
    return pl.pallas_call(
        kernel,
        out_shape=jax.ShapeDtypeStruct(video.shape, video.dtype),
        in_specs=[
            pl.BlockSpec(memory_space=pl.ANY),
            pl.BlockSpec(memory_space=pltpu.VMEM),
            pl.BlockSpec(memory_space=pl.ANY),
        ],
        out_specs=pl.BlockSpec(memory_space=pl.ANY),
        scratch_shapes=[
            pltpu.VMEM((F, R, W, C), BF),
            pltpu.VMEM((F, R, W, C), BF),
            pltpu.VMEM((2, F + 2, R + 2, W, K1), BF),
            pltpu.VMEM((4, 3, 3, 5, LO, C), BF),
            pltpu.VMEM((2, 2, W, C), F32),
            pltpu.VMEM((2, R) + packet, BF),
            pltpu.VMEM((2, R) + packet, BF),
            pltpu.VMEM((2, R) + packet, BF),
            pltpu.VMEM((4, 2, R) + packet, BF),
            pltpu.VMEM((4, R) + packet, BF),
            pltpu.VMEM((4, 2, 2) + packet, BF),
            pltpu.VMEM((4, 2) + packet, BF),
            dma((4, 4)), dma((2,)), dma((2, 2, R)), dma((2, R)),
            dma((2, 2, R)), dma((2, 2, R)),
            dma((4, R)), dma((4, R)),
            dma((4, 2, 2)), dma((4, 2, 2)),
            dma((4, 2)), dma((4, 2)),
        ],
        compiler_params=pltpu.CompilerParams(
            collective_id=0, has_side_effects=True, vmem_limit_bytes=56 << 20),
        name="blocks",
    )(video, gains, kernels)


def solution(mesh):
    in_specs = (P("tm", "rows", None, None), P(), P())
    out_specs = P("tm", "rows", None, None)
    return jax.shard_map(body, mesh=mesh, in_specs=in_specs, out_specs=out_specs, check_vma=False)
```

time: 108 us -> 70.3 us (0.65)
  Pallas kernels: 106 us -> 67.9 us
    pallas_call x1, Pallas kernels: 106 us -> 67.9 us  [body(): pl.pallas_call(kernel, out_shape=jax.ShapeDtypeStruct(video.shape, video....]
where the time goes in v2:
time: 70.3 us; the launch traced here: 70 us
  Pallas kernels  67.9 us (97%)
  local copies, waits for them, and re-layouts  2.06 us (3%)
    pallas_call x1, Pallas kernels, body(): pl.pallas_call(kernel, out_shape=jax.ShapeDtypeStruct(video.shape, video....  67.9 us
    unnamed x1, local copies, waits for them, and re-layouts  2.06 us

profile of v2, /device:TPU:9, one launch (start us, length us, event | category | flops | bytes accessed | tf_op | source)
XLA Modules:
  0.0 70.0 jit_solution(8248951875606253518)
XLA Ops:
  0.0 67.9 %blocks.1 = bf16[4,4,96,192]{3,2,1,0:T(8,128)(2,1)} custom-call(bf16[4,4,96,192]{3,2,1,0:T(8,128)(2,1)} %video.1, f32[4,192]{1,0:T(4,128)} %gains.1, bf16[4,3,3,3,192,192]{5,4,3,2,1,0:T(8,128)(2,1)} %kernels.1), custom_call_target="tpu_custom_call" | custom-call | tf_op jit(solution)/shard_map/blocks/pallas_call | solution.py:414
  68.0 2.1 %copy.5 = bf16[4,4,96,192]{3,2,1,0:T(8,128)(2,1)} copy(bf16[4,4,96,192]{3,2,1,0:T(8,128)(2,1)} %blocks.1) | data formatting | bytes 1179648

commit v3 on v2

--- a/solution.py
+++ b/solution.py
@@ -69,8 +69,8 @@
 
 def kernel(
     video, gains, kernels, out,
-    vid, res, X, Wt, acc, own, swap_out, swap_in, A, T, N, Q,
-    w_sem, v_sem, l_sem, o_sem, sw_send, sw_recv, t_send, t_recv, n_send, n_recv, q_send, q_recv,
+    vid, X, Wt, acc, own, swap_in, A, T, N, Q,
+    w_sem, v_sem, l_sem, sw_send, sw_recv, t_send, t_recv, n_send, n_recv, q_send, q_recv,
 ):
     slab, strip, partner, swaps = place()
     has_prev, has_next = slab > 0, slab < 7
@@ -232,8 +232,7 @@
                 for p in (1, 0):
                     row_copy(j, p, 1 - side).wait_recv()
 
-        @pl.loop(0, 4)
-        def _(i):
+        for i in range(4):
             p, side = lax.div(i, 2), lax.rem(i, 2)
             widen_packet(N.at[j, p, side], j, 2 + 2 * p, 5 * side)
 
@@ -262,8 +261,7 @@
             def _(side=side):
                 corner_copy(j, 1 - side).wait_recv()
 
-        @pl.loop(0, 2)
-        def _(side):
+        for side in range(2):
             widen_packet(Q.at[j, side], j, 0, 5 * side)
 
     def convolve(j, p, rows):
@@ -283,8 +281,7 @@
     def after(j, p, rows):
         @pl.when(lax.rem(j, 2) == 1)
         def _():
-            @pl.loop(0, 2)
-            def _(i):
+            for i in range(2):
                 r = rows[0] + i * (rows[1] - rows[0])
                 old = split(swap_in[p, r])
                 pair = [tuple((a + b).astype(BF).astype(F32) for a, b in zip(old[f], sums(f, i))) for f in range(2)]
@@ -297,13 +294,12 @@
         def _():
             g = gain(j + 1)
 
-            @pl.loop(0, 2)
-            def _(i):
+            for i in range(2):
                 r = rows[0] + i * (rows[1] - rows[0])
                 emit(j + 1, p, r, [norm_act(sums(f, i), g) for f in range(2)])
 
     def outward(p, r):
-        return exchange(swap_in, swap_out, 1, p, r)
+        return exchange(swap_in, out, 1, p, r)
 
     g0 = gain(0)
 
@@ -312,8 +308,7 @@
         p = 1 - q
         finish(exchange(own, swap_in, 0, p))
 
-        @pl.loop(0, R)
-        def _(r):
+        for r in range(R):
             emit(0, p, r, [norm_act(v, g0) for v in split(swap_in[p, r])])
 
         send_rows(0, p)
@@ -326,8 +321,7 @@
         first = jnp.where(jnp.logical_or(u == 1, u == 2), 0, 1)
         return 1 - lax.div(u, 2), (first, 3 - first)
 
-    @pl.loop(0, 4)
-    def _(j):
+    for j in range(4):
         for copy in weights(j):
             copy.wait()
 
@@ -360,19 +354,11 @@
                 for r in rows:
                     begin(outward(p, r))
 
-    def stored(p, r):
-        return pltpu.make_async_copy(res.at[pl.ds(2 * p, 2), r], out.at[pl.ds(2 * p, 2), r], o_sem.at[p, r])
-
-    @pl.loop(0, 8)
-    def _(i):
-        p, rows = unit(lax.div(i, 2))
-        r = rows[0] + lax.rem(i, 2) * (rows[1] - rows[0])
-        finish(outward(p, r))
-        pair = split(swap_out[p, r])
-        for f in range(2):
-            res[2 * p + f, r, :, 0:LO] = pair[f][0].astype(BF)
-            res[2 * p + f, r, :, LO:C] = pair[f][1][:, :HI].astype(BF)
-        stored(p, r).start()
+    @pl.loop(0, 2)
+    def _(p):
+        @pl.loop(0, R)
+        def _(r):
+            finish(outward(p, r))
 
     @pl.when(swaps)
     def _():
@@ -401,19 +387,21 @@
             for r in range(R):
                 frames_copy(j, r).wait_send()
 
-    @pl.loop(0, 2)
-    def _(p):
-        @pl.loop(0, R)
-        def _(r):
-            stored(p, r).wait()
+
+def unpack(packets, out):
+    for r in range(R):
+        pair = split(packets[0, r])
+        for f in range(2):
+            out[f, r, :, 0:LO] = pair[f][0].astype(BF)
+            out[f, r, :, LO:C] = pair[f][1][:, :HI].astype(BF)
 
 
 def body(video, gains, kernels):
     packet = (W, 2 * C)
     dma = pltpu.SemaphoreType.DMA
-    return pl.pallas_call(
+    packets = pl.pallas_call(
         kernel,
-        out_shape=jax.ShapeDtypeStruct(video.shape, video.dtype),
+        out_shape=jax.ShapeDtypeStruct((2, R) + packet, BF),
         in_specs=[
             pl.BlockSpec(memory_space=pl.ANY),
             pl.BlockSpec(memory_space=pltpu.VMEM),
@@ -422,18 +410,16 @@
         out_specs=pl.BlockSpec(memory_space=pl.ANY),
         scratch_shapes=[
             pltpu.VMEM((F, R, W, C), BF),
-            pltpu.VMEM((F, R, W, C), BF),
             pltpu.VMEM((2, F + 2, R + 2, W, K1), BF),
             pltpu.VMEM((4, 3, 3, 5, LO, C), BF),
             pltpu.VMEM((2, 2, W, C), F32),
-            pltpu.VMEM((2, R) + packet, BF),
             pltpu.VMEM((2, R) + packet, BF),
             pltpu.VMEM((2, R) + packet, BF),
             pltpu.VMEM((4, 2, R) + packet, BF),
             pltpu.VMEM((4, R) + packet, BF),
             pltpu.VMEM((4, 2, 2) + packet, BF),
             pltpu.VMEM((4, 2) + packet, BF),
-            dma((4, 4)), dma((2,)), dma((2, 2, R)), dma((2, R)),
+            dma((4, 4)), dma((2,)), dma((2, 2, R)),
             dma((2, 2, R)), dma((2, 2, R)),
             dma((4, R)), dma((4, R)),
             dma((4, 2, 2)), dma((4, 2, 2)),
@@ -443,6 +429,14 @@
             collective_id=0, has_side_effects=True, vmem_limit_bytes=56 << 20),
         name="blocks",
     )(video, gains, kernels)
+    return pl.pallas_call(
+        unpack,
+        out_shape=jax.ShapeDtypeStruct(video.shape, video.dtype),
+        grid=(2,),
+        in_specs=[pl.BlockSpec((1, R) + packet, lambda p: (p, 0, 0, 0))],
+        out_specs=pl.BlockSpec((2, R, W, C), lambda p: (p, 0, 0, 0)),
+        name="unpack",
+    )(packets)
 
 
 def solution(mesh):

time: 70.3 us -> 64.9 us (0.923)
  Pallas kernels: 67.9 us -> 64.8 us
  local copies, waits for them, and re-layouts: 2.06 us -> 0 us
    pallas_call x1 -> x2, Pallas kernels: 67.9 us -> 64.8 us  [the longest x1 62.8 us: body(): pl.pallas_call(kernel, out_shape=jax.ShapeDtypeStruct((2, R) + packet, BF...]
    unnamed x1 -> x0, local copies, waits for them, and re-layouts: 2.06 us -> none
where the time goes in v3:
time: 64.9 us; the launch traced here: 64.8 us
  Pallas kernels  64.8 us (100%)
    pallas_call x1, Pallas kernels, body(): pl.pallas_call(kernel, out_shape=jax.ShapeDtypeStruct((2, R) + packet, BF...  62.8 us
    pallas_call x1, Pallas kernels, body(): pl.pallas_call(unpack, out_shape=jax.ShapeDtypeStruct(video.shape, video....  1.94 us

profile of v3, /device:TPU:9, one launch (start us, length us, event | category | flops | bytes accessed | tf_op | source)
XLA Modules:
  0.0 64.8 jit_solution(17459268424905047190)
XLA Ops:
  0.0 62.8 %blocks.1.packets = bf16[2,4,96,384]{3,2,1,0:T(8,128)(2,1)} custom-call(bf16[4,4,96,192]{3,2,1,0:T(8,128)(2,1)} %video.1, f32[4,192]{1,0:T(4,128)} %gains.1, bf16[4,3,3,3,192,192]{5,4,3,2,1,0:T(8,128)(2,1)} %kernels.1), custom_call_target="tpu_custom_call" | custom-call | tf_op jit(solution)/shard_map/blocks/pallas_call | solution.py:402
  62.8 1.9 %unpack.1 = bf16[4,4,96,192]{3,2,1,0:T(8,128)(2,1)} custom-call(bf16[2,4,96,384]{3,2,1,0:T(8,128)(2,1)} %blocks.1.packets), custom_call_target="tpu_custom_call" | custom-call | tf_op jit(solution)/shard_map/unpack/pallas_call | solution.py:432

commit v4 on v3

--- a/solution.py
+++ b/solution.py
@@ -329,10 +329,13 @@
         def _(u):
             p, rows = unit(u)
 
+            @pl.when(u == jnp.where(j == 0, 1, 0))
+            def _():
+                forward_corners(j)
+
             @pl.when(u == 1)
             def _():
                 take_rows(j)
-                forward_corners(j)
 
             @pl.when(u == 2)
             def _():

time: 64.9 us -> 59.9 us (0.923); the launches traced: 64.8 us -> 58.7 us
  Pallas kernels: 64.8 us -> 58.7 us
    pallas_call x1, Pallas kernels: 62.8 us -> 56.8 us  [body(): pl.pallas_call(kernel, out_shape=jax.ShapeDtypeStruct((2, R) + packet, BF...]
where the time goes in v4:
time: 59.9 us; the launch traced here: 58.7 us
  Pallas kernels  58.7 us (98%)
    pallas_call x1, Pallas kernels, body(): pl.pallas_call(kernel, out_shape=jax.ShapeDtypeStruct((2, R) + packet, BF...  56.8 us
    pallas_call x1, Pallas kernels, body(): pl.pallas_call(unpack, out_shape=jax.ShapeDtypeStruct(video.shape, video....  1.94 us

profile of v4, /device:TPU:9, one launch (start us, length us, event | category | flops | bytes accessed | tf_op | source)
XLA Modules:
  0.0 58.7 jit_solution(2295048477584190477)
XLA Ops:
  0.0 56.8 %blocks.1.packets = bf16[2,4,96,384]{3,2,1,0:T(8,128)(2,1)} custom-call(bf16[4,4,96,192]{3,2,1,0:T(8,128)(2,1)} %video.1, f32[4,192]{1,0:T(4,128)} %gains.1, bf16[4,3,3,3,192,192]{5,4,3,2,1,0:T(8,128)(2,1)} %kernels.1), custom_call_target="tpu_custom_call" | custom-call | tf_op jit(solution)/shard_map/blocks/pallas_call | solution.py:405
  56.8 1.9 %unpack.1 = bf16[4,4,96,192]{3,2,1,0:T(8,128)(2,1)} custom-call(bf16[2,4,96,384]{3,2,1,0:T(8,128)(2,1)} %blocks.1.packets), custom_call_target="tpu_custom_call" | custom-call | tf_op jit(solution)/shard_map/unpack/pallas_call | solution.py:435

commit v5 on v4

--- a/solution.py
+++ b/solution.py
@@ -171,8 +171,7 @@
         @pl.loop(0, R)
         def _(r, p=p):
             packed(r, p)
-
-        begin(exchange(own, swap_in, 0, p))
+            begin(exchange(own, swap_in, 0, p, r))
 
     for copy in weights(0):
         copy.start()
@@ -306,9 +305,8 @@
     @pl.loop(0, 2)
     def _(q):
         p = 1 - q
-        finish(exchange(own, swap_in, 0, p))
-
         for r in range(R):
+            finish(exchange(own, swap_in, 0, p, r))
             emit(0, p, r, [norm_act(v, g0) for v in split(swap_in[p, r])])
 
         send_rows(0, p)
@@ -367,10 +365,9 @@
     def _():
         @pl.loop(0, 2)
         def _(p):
-            exchange(own, swap_in, 0, p)[0].wait_send()
-
             @pl.loop(0, R)
             def _(r):
+                exchange(own, swap_in, 0, p, r)[0].wait_send()
                 outward(p, r)[0].wait_send()
 
     @pl.loop(0, 4)

time: 59.9 us -> 58.3 us (0.973)
  Pallas kernels: 58.7 us -> 57.2 us
    pallas_call x1, Pallas kernels: 56.8 us -> 55.3 us  [body(): pl.pallas_call(kernel, out_shape=jax.ShapeDtypeStruct((2, R) + packet, BF...]
where the time goes in v5:
time: 58.3 us; the launch traced here: 57.2 us
  Pallas kernels  57.2 us (98%)
    pallas_call x1, Pallas kernels, body(): pl.pallas_call(kernel, out_shape=jax.ShapeDtypeStruct((2, R) + packet, BF...  55.3 us
    pallas_call x1, Pallas kernels, body(): pl.pallas_call(unpack, out_shape=jax.ShapeDtypeStruct(video.shape, video....  1.94 us

profile of v5, /device:TPU:9, one launch (start us, length us, event | category | flops | bytes accessed | tf_op | source)
XLA Modules:
  0.0 57.2 jit_solution(7187376045311534063)
XLA Ops:
  0.0 55.3 %blocks.1.packets = bf16[2,4,96,384]{3,2,1,0:T(8,128)(2,1)} custom-call(bf16[4,4,96,192]{3,2,1,0:T(8,128)(2,1)} %video.1, f32[4,192]{1,0:T(4,128)} %gains.1, bf16[4,3,3,3,192,192]{5,4,3,2,1,0:T(8,128)(2,1)} %kernels.1), custom_call_target="tpu_custom_call" | custom-call | tf_op jit(solution)/shard_map/blocks/pallas_call | solution.py:402
  55.3 1.9 %unpack.1 = bf16[4,4,96,192]{3,2,1,0:T(8,128)(2,1)} custom-call(bf16[2,4,96,384]{3,2,1,0:T(8,128)(2,1)} %blocks.1.packets), custom_call_target="tpu_custom_call" | custom-call | tf_op jit(solution)/shard_map/unpack/pallas_call | solution.py:432
